TPU v7x, 256 devices: a whole 4x4x8 slice. The times are simulated.
256 devices in a mesh: row: 16 (over z_hi, y, core), col: 16 (over x, z_lo).
Axes of the slice: x: 4, y: 4, z: 8 (z_hi: 2, z_lo: 4; z = z_hi * 4 + z_lo), core: 2. Of those that a mesh axis runs over, the one named last changes fastest.
Arguments:
- act_sketch: bfloat16 [2, 8192, 256], P(None, 'row'), may hold values from -6 to 6
- grad_sketch: bfloat16 [2, 8192, 256], P(None, 'row'), may hold values from -6 to 6
- targets: float32 [8192, 256], P('row'), may hold values from -6 to 6
Outputs:
- residual: float32 [8192, 256], P(('row', 'col'))
All inputs are finite; a program needn't handle non-finite values.
Results may differ from a plain program's by a relative error of at most 0.014.
The roundings to bfloat16 on the way count: a program that leaves them out, or rounds other values in their place, can miss the bound.
Values may be sent and summed in bfloat16 or wider, within the bound.
A program may use at most 64 MiB of HBM per device.

v0:
```python
import math

import jax
import jax.numpy as jnp
from jax import lax
from jax.sharding import PartitionSpec as P

ITERS = 8


def broadcast(value, axis, source):
    kept = jnp.where(lax.axis_index(axis) == source, value, 0).astype(value.dtype)
    return lax.psum(kept, axis)


def spread(panel, root):
    return broadcast(panel, "row", root)


def gram_pair(left, right):
    return lax.dot_general(
        left, right, (((1,), (1,)), ((), ())), preferred_element_type=jnp.float32
    )


def body(act_sketch, grad_sketch, targets):
    row_count = lax.axis_size("row")
    col_count = lax.axis_size("col")
    ratio = col_count // row_count
    examples = targets.shape[0]
    col_block = examples // ratio
    share_rows = examples // col_count
    col_place = lax.axis_index("col")
    root = col_place // ratio
    scale = act_sketch.shape[2] * math.sqrt(examples * row_count) / 4.0
    act_cols, grad_cols = (broadcast(act_sketch, "row", root), broadcast(grad_sketch, "row", root))
    total = jnp.zeros((examples, col_block), jnp.float32)
    for layer in range(act_sketch.shape[0]):
        act_gram = gram_pair(act_sketch[layer], act_cols[layer])
        grad_gram = gram_pair(grad_sketch[layer], grad_cols[layer])
        total = total + act_gram * grad_gram
    kernel = (total / scale).astype(jnp.bfloat16)
    share = lax.dynamic_slice_in_dim(targets, col_place * share_rows, share_rows, 0)
    for step in range(ITERS):
        squashed = jnp.tanh(share).astype(jnp.bfloat16)
        gathered = lax.all_gather(squashed, "col", axis=0, tiled=True)
        panel = spread(gathered, root)
        partial_value = jnp.dot(kernel, panel, preferred_element_type=jnp.float32)
        piece = lax.psum_scatter(partial_value, "col", scatter_dimension=0, tiled=True)
        share = share - 0.05 * piece
    return share


def solution(mesh):
    return jax.shard_map(
        body,
        mesh=mesh,
        in_specs=(P(None, "row", None), P(None, "row", None), P("row", None)),
        out_specs=P(("row", "col"), None),
        check_vma=False,
    )
```

profile of v0, /device:TPU:1, one launch (start us, length us, event | category | flops | bytes accessed | tf_op | source)
XLA Modules:
  0.0 2469.9 jit_solution(18417355909062240451)
XLA Ops:
  6.5 0.8 tanh_convert_fusion.7
  7.4 39.2 %all_gather.24 = bf16[512,256]{1,0:T(8,128)(2,1)S(1)} all-gather(bf16[32,256]{1,0:T(8,128)(2,1)S(1)} %tanh_convert_fusion.7), channel_id=1, replica_groups=mesh['row'=16,'col'=16] {'col'}, dimensions={0}, use_global_device_ids=true | all-gather | bytes 278528 | tf_op jit(solution)/shard_map/all_gather | solution.py:46
  46.6 0.7 broadcast_select_fusion.9
  47.3 1.1 broadcast_select_fusion
  48.4 0.0 reduce-scatter.9.cloned.1.call-start
  48.4 187.0 %all-reduce.24.cloned.1.call-done = (bf16[2,512,256]{2,1,0:T(8,128)(2,1)}, bf16[2,512,256]{2,1,0:T(8,128)(2,1)}, bf16[512,256]{1,0:T(8,128)(2,1)}) async-done(((bf16[2,512,256]{2,1,0:T(8,128)(2,1)}, bf16[2,512,256]{2,1,0:T(8,128)(2,1)}, bf16[512,256]{1,0:T(8,128)(2,1)}), (bf16[2,512,256]{2,1,0:T(8,128)(2,1)}, bf16[2,512,256]{2,1,0:T(8,128)(2,1)}, bf16[512,256]{1,0:T(8,128)(2,1)})) %all-reduce.24.cloned.1.call-update) | async-done | bytes 1310736 | tf_op jit(solution)/shard_map/psum | solution.py:13
  235.5 1.3 fusion.3
  236.8 0.3 fusion.4
  237.2 0.7 copy-done.2
  237.9 0.3 convolution_multiply_fusion.1
  238.2 0.3 fusion.2
  238.5 0.6 copy-done.5
  239.1 1.1 fusion.13
  240.3 75.8 %reduce-scatter.9.cloned.1.call-done = f32[32,256]{1,0:T(8,128)} async-done(((f32[512,256]{1,0:T(8,128)}), f32[32,256]{1,0:T(8,128)}) %reduce-scatter.9.cloned.1.call-update) | async-done | bytes 32784 | tf_op jit(solution)/shard_map/reduce_scatter | solution.py:49
  316.2 0.8 tanh_convert_fusion.6
  317.0 32.5 %all_gather.25 = bf16[512,256]{1,0:T(8,128)(2,1)S(1)} all-gather(bf16[32,256]{1,0:T(8,128)(2,1)S(1)} %get-tuple-element.12), channel_id=1, replica_groups=mesh['row'=16,'col'=16] {'col'}, dimensions={0}, use_global_device_ids=true | all-gather | bytes 278528 | tf_op jit(solution)/shard_map/all_gather | solution.py:46
  349.5 0.7 broadcast_select_fusion.8
  350.2 0.0 reduce-scatter.11.cloned.1.call-start
  350.3 194.6 %all-reduce.10.cloned.1.call-done = bf16[512,256]{1,0:T(8,128)(2,1)} async-done(((bf16[512,256]{1,0:T(8,128)(2,1)}), bf16[512,256]{1,0:T(8,128)(2,1)}) %all-reduce.10.cloned.1.call-update) | async-done | bytes 262160 | tf_op jit(solution)/shard_map/psum | solution.py:13
  544.9 2.1 fusion.14
  547.0 0.0 all-reduce.12.cloned.1.call-start
  547.0 75.9 %reduce-scatter.11.cloned.1.call-done = f32[32,256]{1,0:T(8,128)} async-done(((f32[512,256]{1,0:T(8,128)}), f32[32,256]{1,0:T(8,128)}) %reduce-scatter.11.cloned.1.call-update) | async-done | bytes 32784 | tf_op jit(solution)/shard_map/reduce_scatter | solution.py:49
  622.9 0.8 tanh_convert_fusion.5
  623.7 32.5 %all_gather.26 = bf16[512,256]{1,0:T(8,128)(2,1)S(1)} all-gather(bf16[32,256]{1,0:T(8,128)(2,1)S(1)} %tanh_convert_fusion.5), channel_id=1, replica_groups=mesh['row'=16,'col'=16] {'col'}, dimensions={0}, use_global_device_ids=true | all-gather | bytes 278528 | tf_op jit(solution)/shard_map/all_gather | solution.py:46
  656.1 0.7 broadcast_select_fusion.7
  656.9 0.0 reduce-scatter.13.cloned.1.call-start
  656.9 194.4 %all-reduce.12.cloned.1.call-done = bf16[512,256]{1,0:T(8,128)(2,1)} async-done(((bf16[512,256]{1,0:T(8,128)(2,1)}), bf16[512,256]{1,0:T(8,128)(2,1)}) %all-reduce.12.cloned.1.call-update) | async-done | bytes 262160 | tf_op jit(solution)/shard_map/psum | solution.py:13
  851.3 2.1 fusion.15
  853.4 0.0 all-reduce.14.cloned.1.call-start
  853.5 75.9 %reduce-scatter.13.cloned.1.call-done = f32[32,256]{1,0:T(8,128)} async-done(((f32[512,256]{1,0:T(8,128)}), f32[32,256]{1,0:T(8,128)}) %reduce-scatter.13.cloned.1.call-update) | async-done | bytes 32784 | tf_op jit(solution)/shard_map/reduce_scatter | solution.py:49
  929.3 0.8 tanh_convert_fusion.4
  930.1 32.5 %all_gather.27 = bf16[512,256]{1,0:T(8,128)(2,1)S(1)} all-gather(bf16[32,256]{1,0:T(8,128)(2,1)S(1)} %get-tuple-element.10), channel_id=1, replica_groups=mesh['row'=16,'col'=16] {'col'}, dimensions={0}, use_global_device_ids=true | all-gather | bytes 278528 | tf_op jit(solution)/shard_map/all_gather | solution.py:46
  962.6 0.7 broadcast_select_fusion.6
  963.4 194.4 %all-reduce.14.cloned.1.call-done = bf16[512,256]{1,0:T(8,128)(2,1)} async-done(((bf16[512,256]{1,0:T(8,128)(2,1)}), bf16[512,256]{1,0:T(8,128)(2,1)}) %all-reduce.14.cloned.1.call-update) | async-done | bytes 262160 | tf_op jit(solution)/shard_map/psum | solution.py:13
  1157.8 2.1 fusion.16
  1159.9 76.0 %reduce-scatter.15.cloned.1.call-done = f32[32,256]{1,0:T(8,128)} async-done(((f32[512,256]{1,0:T(8,128)}), f32[32,256]{1,0:T(8,128)}) %reduce-scatter.15.cloned.1.call-update) | async-done | bytes 32784 | tf_op jit(solution)/shard_map/reduce_scatter | solution.py:49
  1235.9 0.8 tanh_convert_fusion.3
  1236.7 32.5 %all_gather.28 = bf16[512,256]{1,0:T(8,128)(2,1)S(1)} all-gather(bf16[32,256]{1,0:T(8,128)(2,1)S(1)} %tanh_convert_fusion.3), channel_id=1, replica_groups=mesh['row'=16,'col'=16] {'col'}, dimensions={0}, use_global_device_ids=true | all-gather | bytes 278528 | tf_op jit(solution)/shard_map/all_gather | solution.py:46
  1269.2 0.7 broadcast_select_fusion.5
  1270.0 194.6 %all-reduce.16.cloned.1.call-done = bf16[512,256]{1,0:T(8,128)(2,1)} async-done(((bf16[512,256]{1,0:T(8,128)(2,1)}), bf16[512,256]{1,0:T(8,128)(2,1)}) %all-reduce.16.cloned.1.call-update) | async-done | bytes 262160 | tf_op jit(solution)/shard_map/psum | solution.py:13
  1464.6 2.1 fusion.17
  1466.7 0.0 all-reduce.18.cloned.1.call-start
  1466.8 75.9 %reduce-scatter.17.cloned.1.call-done = f32[32,256]{1,0:T(8,128)} async-done(((f32[512,256]{1,0:T(8,128)}), f32[32,256]{1,0:T(8,128)}) %reduce-scatter.17.cloned.1.call-update) | async-done | bytes 32784 | tf_op jit(solution)/shard_map/reduce_scatter | solution.py:49
  1542.6 0.8 tanh_convert_fusion.2
  1543.4 32.5 %all_gather.29 = bf16[512,256]{1,0:T(8,128)(2,1)S(1)} all-gather(bf16[32,256]{1,0:T(8,128)(2,1)S(1)} %get-tuple-element.8), channel_id=1, replica_groups=mesh['row'=16,'col'=16] {'col'}, dimensions={0}, use_global_device_ids=true | all-gather | bytes 278528 | tf_op jit(solution)/shard_map/all_gather | solution.py:46
  1575.9 0.7 broadcast_select_fusion.4
  1576.7 194.4 %all-reduce.18.cloned.1.call-done = bf16[512,256]{1,0:T(8,128)(2,1)} async-done(((bf16[512,256]{1,0:T(8,128)(2,1)}), bf16[512,256]{1,0:T(8,128)(2,1)}) %all-reduce.18.cloned.1.call-update) | async-done | bytes 262160 | tf_op jit(solution)/shard_map/psum | solution.py:13
  1771.0 2.1 fusion.18
  1773.2 75.9 %reduce-scatter.19.cloned.1.call-done = f32[32,256]{1,0:T(8,128)} async-done(((f32[512,256]{1,0:T(8,128)}), f32[32,256]{1,0:T(8,128)}) %reduce-scatter.19.cloned.1.call-update) | async-done | bytes 32784 | tf_op jit(solution)/shard_map/reduce_scatter | solution.py:49
  1849.1 0.8 tanh_convert_fusion.1
  1849.8 32.5 %all_gather.30 = bf16[512,256]{1,0:T(8,128)(2,1)S(1)} all-gather(bf16[32,256]{1,0:T(8,128)(2,1)S(1)} %tanh_convert_fusion.1), channel_id=1, replica_groups=mesh['row'=16,'col'=16] {'col'}, dimensions={0}, use_global_device_ids=true | all-gather | bytes 278528 | tf_op jit(solution)/shard_map/all_gather | solution.py:46
  1882.3 0.7 broadcast_select_fusion.3
  1883.1 0.0 reduce-scatter.21.cloned.1.call-start
  1883.1 194.4 %all-reduce.20.cloned.1.call-done = bf16[512,256]{1,0:T(8,128)(2,1)} async-done(((bf16[512,256]{1,0:T(8,128)(2,1)}), bf16[512,256]{1,0:T(8,128)(2,1)}) %all-reduce.20.cloned.1.call-update) | async-done | bytes 262160 | tf_op jit(solution)/shard_map/psum | solution.py:13
  2077.5 2.1 fusion.19
  2079.7 75.9 %reduce-scatter.21.cloned.1.call-done = f32[32,256]{1,0:T(8,128)} async-done(((f32[512,256]{1,0:T(8,128)}), f32[32,256]{1,0:T(8,128)}) %reduce-scatter.21.cloned.1.call-update) | async-done | bytes 32784 | tf_op jit(solution)/shard_map/reduce_scatter | solution.py:49
  2155.5 0.8 tanh_convert_fusion
  2156.3 32.5 %all_gather.31 = bf16[512,256]{1,0:T(8,128)(2,1)S(1)} all-gather(bf16[32,256]{1,0:T(8,128)(2,1)S(1)} %tanh_convert_fusion), channel_id=1, replica_groups=mesh['row'=16,'col'=16] {'col'}, dimensions={0}, use_global_device_ids=true | all-gather | bytes 278528 | tf_op jit(solution)/shard_map/all_gather | solution.py:46
  2188.8 0.7 broadcast_select_fusion.2
  2189.5 0.0 reduce-scatter.23.cloned.1.call-start
  2189.6 194.4 %all-reduce.22.cloned.1.call-done = bf16[512,256]{1,0:T(8,128)(2,1)} async-done(((bf16[512,256]{1,0:T(8,128)(2,1)}), bf16[512,256]{1,0:T(8,128)(2,1)}) %all-reduce.22.cloned.1.call-update) | async-done | bytes 262160 | tf_op jit(solution)/shard_map/psum | solution.py:13
  2384.0 2.1 fusion.20
  2386.1 75.9 %reduce-scatter.23.cloned.1.call-done = f32[32,256]{1,0:T(8,128)} async-done(((f32[512,256]{1,0:T(8,128)}), f32[32,256]{1,0:T(8,128)}) %reduce-scatter.23.cloned.1.call-update) | async-done | bytes 32784 | tf_op jit(solution)/shard_map/reduce_scatter | solution.py:49
  2462.0 1.4 multiply_subtract_fusion
  (40 shorter events, 0.6 us)
Async XLA Ops:
  6.5 40.8 %copy-start = (bf16[2,512,256]{2,1,0:T(8,128)(2,1)S(1)}, bf16[2,512,256]{2,1,0:T(8,128)(2,1)}, u32[]{:S(2)}) copy-start(bf16[2,512,256]{2,1,0:T(8,128)(2,1)} %param.4) | copy-start | bytes 1572868
  6.5 228.9 %all-reduce.24.cloned.1.call-start = ((), (), s32[]{:S(2)}) async-start(), calls=%async_computation.23 | async-start | bytes 2621440 | tf_op jit(solution)/shard_map/psum | solution.py:13
  48.4 187.1 %copy-start.1 = (bf16[2,512,256]{2,1,0:T(8,128)(2,1)S(1)}, bf16[2,512,256]{2,1,0:T(8,128)(2,1)}, u32[]{:S(2)}) copy-start(bf16[2,512,256]{2,1,0:T(8,128)(2,1)} %param.3) | copy-start | bytes 1572868
  48.4 267.8 %reduce-scatter.9.cloned.1.call-start = ((), (), s32[]{:S(2)}) async-start(), calls=%async_computation.8 | async-start | bytes 557056 | tf_op jit(solution)/shard_map/reduce_scatter | solution.py:49
  235.5 1.4 copy-start.3
  236.8 1.0 copy-start.2
  238.2 1.0 copy-start.5
  240.3 304.6 %all-reduce.10.cloned.1.call-start = ((), (), s32[]{:S(2)}) async-start(), calls=%async_computation.9 | async-start | bytes 524288 | tf_op jit(solution)/shard_map/psum | solution.py:13
  350.2 272.7 %reduce-scatter.11.cloned.1.call-start = ((), (), s32[]{:S(2)}) async-start(), calls=%async_computation.10 | async-start | bytes 557056 | tf_op jit(solution)/shard_map/reduce_scatter | solution.py:49
  547.0 304.3 %all-reduce.12.cloned.1.call-start = ((), (), s32[]{:S(2)}) async-start(), calls=%async_computation.11 | async-start | bytes 524288 | tf_op jit(solution)/shard_map/psum | solution.py:13
  656.9 272.5 %reduce-scatter.13.cloned.1.call-start = ((), (), s32[]{:S(2)}) async-start(), calls=%async_computation.12 | async-start | bytes 557056 | tf_op jit(solution)/shard_map/reduce_scatter | solution.py:49
  853.4 75.9 %copy-start.7 = (f32[32,256]{1,0:T(8,128)S(1)}, f32[32,256]{1,0:T(8,128)}, u32[]{:S(2)}) copy-start(f32[32,256]{1,0:T(8,128)} %reduce-scatter.11.cloned.1.call-done) | copy-start | bytes 98308
  853.4 304.3 %all-reduce.14.cloned.1.call-start = ((), (), s32[]{:S(2)}) async-start(), calls=%async_computation.13 | async-start | bytes 524288 | tf_op jit(solution)/shard_map/psum | solution.py:13
  963.3 272.6 %reduce-scatter.15.cloned.1.call-start = ((), (), s32[]{:S(2)}) async-start(), calls=%async_computation.14 | async-start | bytes 557056 | tf_op jit(solution)/shard_map/reduce_scatter | solution.py:49
  1159.9 304.7 %all-reduce.16.cloned.1.call-start = ((), (), s32[]{:S(2)}) async-start(), calls=%async_computation.15 | async-start | bytes 524288 | tf_op jit(solution)/shard_map/psum | solution.py:13
  1270.0 272.7 %reduce-scatter.17.cloned.1.call-start = ((), (), s32[]{:S(2)}) async-start(), calls=%async_computation.16 | async-start | bytes 557056 | tf_op jit(solution)/shard_map/reduce_scatter | solution.py:49
  1466.7 75.9 %copy-start.8 = (f32[32,256]{1,0:T(8,128)S(1)}, f32[32,256]{1,0:T(8,128)}, u32[]{:S(2)}) copy-start(f32[32,256]{1,0:T(8,128)} %reduce-scatter.15.cloned.1.call-done) | copy-start | bytes 98308
  1466.7 304.3 %all-reduce.18.cloned.1.call-start = ((), (), s32[]{:S(2)}) async-start(), calls=%async_computation.17 | async-start | bytes 524288 | tf_op jit(solution)/shard_map/psum | solution.py:13
  1576.6 272.4 %reduce-scatter.19.cloned.1.call-start = ((), (), s32[]{:S(2)}) async-start(), calls=%async_computation.18 | async-start | bytes 557056 | tf_op jit(solution)/shard_map/reduce_scatter | solution.py:49
  1773.2 304.3 %all-reduce.20.cloned.1.call-start = ((), (), s32[]{:S(2)}) async-start(), calls=%async_computation.19 | async-start | bytes 524288 | tf_op jit(solution)/shard_map/psum | solution.py:13
  1883.1 272.5 %reduce-scatter.21.cloned.1.call-start = ((), (), s32[]{:S(2)}) async-start(), calls=%async_computation.20 | async-start | bytes 557056 | tf_op jit(solution)/shard_map/reduce_scatter | solution.py:49
  2079.6 75.9 %copy-start.4 = (f32[32,256]{1,0:T(8,128)S(1)}, f32[32,256]{1,0:T(8,128)}, u32[]{:S(2)}) copy-start(f32[32,256]{1,0:T(8,128)} %reduce-scatter.19.cloned.1.call-done) | copy-start | bytes 98308
  2079.6 304.4 %all-reduce.22.cloned.1.call-start = ((), (), s32[]{:S(2)}) async-start(), calls=%async_computation.21 | async-start | bytes 524288 | tf_op jit(solution)/shard_map/psum | solution.py:13
  2189.5 272.5 %reduce-scatter.23.cloned.1.call-start = ((), (), s32[]{:S(2)}) async-start(), calls=%async_computation.22 | async-start | bytes 557056 | tf_op jit(solution)/shard_map/reduce_scatter | solution.py:49
  2386.0 75.9 %copy-start.6 = (f32[32,256]{1,0:T(8,128)S(1)}, f32[32,256]{1,0:T(8,128)}, u32[]{:S(2)}) copy-start(f32[32,256]{1,0:T(8,128)} %reduce-scatter.21.cloned.1.call-done) | copy-start | bytes 98308
Sparse Core Ops, SparseCore 0:
  48.5 186.8 all-reduce.23
  240.4 75.7 reduce-scatter.8
  350.3 194.4 all-reduce.9
  547.2 75.6 reduce-scatter.10
  657.0 194.2 all-reduce.11
  853.7 75.6 reduce-scatter.12
  963.5 194.2 all-reduce.13
  1160.3 75.6 reduce-scatter.14
  1270.1 194.4 all-reduce.15
  1466.9 75.6 reduce-scatter.16
  1576.8 194.2 all-reduce.17
  1773.4 75.6 reduce-scatter.18
  1883.2 194.2 all-reduce.19
  2079.8 75.6 reduce-scatter.20
  2189.6 194.2 all-reduce.21
  2386.3 75.6 reduce-scatter.22
where the time goes:
time: 2480 us; the launch traced here: 2470 us
  waiting for transfers between devices  2160 us (87%)
  blocking collectives  267 us (11%)
    psum x8, waiting for transfers between devices, broadcast(): return lax.psum(kept, axis)  1550 us
    reduce_scatter x8, waiting for transfers between devices, body(): lax.psum_scatter(partial_value, 'col', scatter_dimension=0, tiled=True)  607 us
    all_gather x8, blocking collectives, body(): gathered = lax.all_gather(squashed, 'col', axis=0, tiled=True)  267 us
  transfers between devices with their start and end apart: 16, of which 16 were waited for; matrix products, arithmetic and copies ran while one was open for 0% of the time, Pallas kernels for 0%

commit v1 on v0

v1 whole, which is shorter than its diff:
```python
import functools
import math

import jax
import jax.numpy as jnp
from jax import lax
from jax.experimental import pallas as pl
from jax.experimental.pallas import tpu as pltpu
from jax.sharding import PartitionSpec as P

ITERS = 8
CHUNKS = 4
RATE = 0.05
MESH = pl.DeviceIdType.MESH


def place(x, y, z, k):
    return ((z // 4) * 8 + y * 2 + k, x * 4 + z % 4)


def kernel(inv_scale, act, grad, tgt, out, ra, rg, ca, cg, kt, xbuf, rsend, rrecv, acc, yloc, res, tbuf, sq, osend, orecv,
           lsem, zs, zr, ts, tr, xs, xr, ys, yr, fs, fr, rss, rsr, ags, agr, oss, osr):
    row, col = lax.axis_index("row"), lax.axis_index("col")
    x, zlo = col // 4, col % 4
    hi, y, k = row // 8, (row // 2) % 4, row % 2
    z = hi * 4 + zlo
    zb = z % 2
    q = z // 2
    lo = 1 - hi
    s_me = 2 * x + zb
    j_me = 2 * y + k
    sketches = ((act, ra, ca), (grad, rg, cg))

    def at(dx=0, dy=0, dzb=0, dk=0):
        return place((x + dx) % 4, (y + dy) % 4, z + dzb * (1 - 2 * zb), k + dk * (1 - 2 * k))

    def remote(src, dst, ssem, rsem, device):
        return pltpu.make_async_remote_copy(
            src_ref=src, dst_ref=dst, send_sem=ssem, recv_sem=rsem, device_id=device, device_id_type=MESH)

    local = []
    for n, (src, r, c) in enumerate(sketches):
        local.append(pltpu.make_async_copy(src, r.at[:, :, hi], lsem.at[0, n]))
        local.append(pltpu.make_async_copy(src.at[:, s_me], c.at[:, j_me, hi], lsem.at[1, n]))
    tcols = pl.ds(pl.multiple_of((q // 2) * 128, 128), 128)
    tlocal = pltpu.make_async_copy(tgt.at[s_me, :, tcols], tbuf.at[hi], lsem.at[2, 0])
    for c in local:
        c.start()
    tlocal.start()

    sums = [(dx, dz) for dx in (2, 1, 3, 0) for dz in (1, 0) if (dx, dz) != (0, 0)]
    gathers = [(dy, dk) for dy in (2, 1, 3, 0) for dk in (1, 0) if (dy, dk) != (0, 0)]
    barrier = pltpu.get_barrier_semaphore()

    def greet(device):
        pl.semaphore_signal(barrier, inc=1, device_id=device, device_id_type=MESH)

    for dx, dz in sums:
        greet(at(dx=dx, dzb=dz))
    for dy, dk in gathers:
        greet(at(dy=dy, dk=dk))
    for n in range(1, 4):
        for b in range(2):
            greet(place(x, y, 2 * ((q + n) % 4) + b, k))
    pl.semaphore_wait(barrier, len(sums) + len(gathers) + 6)

    mirror = place(x, y, 7 - z, k)
    s_mirror = 2 * x + 1 - zb
    mcols = pl.ds(pl.multiple_of(((3 - q) // 2) * 128, 128), 128)
    tcopy = remote(tgt.at[s_mirror, :, mcols], tbuf.at[hi], ts, tr, mirror)
    tcopy.start()
    zc = []
    mine = pl.ds(2 * x, 2)
    rows_of = [pl.ds(c * (64 // CHUNKS), 64 // CHUNKS) for c in range(CHUNKS)]
    for chunk, i in enumerate(rows_of):
        zc.append([remote(src.at[:, mine, i], r.at[:, mine, hi, i], zs.at[chunk, n], zr.at[chunk, n], mirror)
                   for n, (src, r, c) in enumerate(sketches)])
    for c in zc[0]:
        c.start()
    yc, fc, xc = {}, {}, {}
    everything = pl.ds(0, 64)

    def forward(dy, part, half, i=everything):
        j = 2 * ((y - dy) % 4) + k
        fc[dy, part] = []
        for n, (src, r, c) in enumerate(sketches):
            if dy == 0:
                source = src.at[:, s_me, i] if part == 0 else r.at[:, s_me, lo, i]
            else:
                source = c.at[:, j, half, i]
            fc[dy, part].append(remote(source, c.at[:, j, half, i], fs.at[dy, part, n], fr.at[dy, part, n], at(dk=1)))
        for c in fc[dy, part]:
            c.start()

    def columns(part, half, i=everything):
        for dy in (2, 1, 3):
            yc[dy, part] = []
            for n, (src, r, c) in enumerate(sketches):
                source = src.at[:, s_me, i] if part == 0 else r.at[:, s_me, lo, i]
                yc[dy, part].append(remote(
                    source, c.at[:, j_me, half, i], ys.at[dy - 1, part, n], yr.at[dy - 1, part, n], at(dy=dy)))
            for c in yc[dy, part]:
                c.start()

    def rows(dx, chunk):
        i = rows_of[chunk]
        xc[dx, chunk] = [remote(r.at[:, mine, lo, i], r.at[:, mine, lo, i], xs.at[dx - 1, chunk, n], xr.at[dx - 1, chunk, n],
                                at(dx=dx)) for n, (src, r, c) in enumerate(sketches)]
        for c in xc[dx, chunk]:
            c.start()

    columns(0, hi)
    for chunk in zc[1:]:
        for c in chunk:
            c.start()
    forward(0, 0, hi)

    tlocal.wait()
    tcopy.wait_recv()
    sq[...] = tbuf[...].reshape(128, 128).T
    half_at = pl.multiple_of((q % 2) * 64, 64)
    res[...] = sq[pl.ds(half_at, 64), :]
    jcols = pl.ds(pl.multiple_of(j_me * 128, 128), 128)

    def gather(p):
        xbuf[p, :, jcols] = jnp.tanh(res[...]).astype(jnp.bfloat16)
        copies = [remote(xbuf.at[p, :, jcols], xbuf.at[p, :, jcols], ags.at[p, n], agr.at[p, n], at(dy=dy, dk=dk))
                  for n, (dy, dk) in enumerate(gathers)]
        for c in copies:
            c.start()
        return copies

    first = gather(0)

    for chunk, i in enumerate(rows_of):
        for c in zc[chunk]:
            c.wait_recv()
        columns(1 + chunk, lo, i)
        rows(1, chunk)
        rows(3, chunk)
        if chunk:
            rows(2, chunk - 1)
        forward(0, 1 + chunk, lo, i)
        if chunk == 1:
            for dy in (1, 3, 2):
                for c in yc[dy, 0]:
                    c.wait_recv()
                forward(dy, 0, hi)
    rows(2, CHUNKS - 1)
    for n, (src, r, c) in enumerate(sketches):
        own = pltpu.make_async_copy(r.at[:, s_me, lo], c.at[:, j_me, lo], lsem.at[3, n])
        own.start()
        local.append(own)
    for chunk, i in enumerate(rows_of):
        for dy in (1, 3, 2):
            for c in yc[dy, 1 + chunk]:
                c.wait_recv()
            forward(dy, 1 + chunk, lo, i)
    for c in local:
        c.wait()
    for group in fc.values():
        for c in group:
            c.wait_recv()

    for dx in (0, 1, 3, 2):
        if dx:
            for chunk in range(CHUNKS):
                for c in xc[dx, chunk]:
                    c.wait_recv()
        quarter = (x - dx) % 4
        lanes = pl.ds(pl.multiple_of(quarter * 256, 256), 256)

        def block(m, _):
            total = jnp.zeros((256, 256), jnp.float32)
            for layer in range(2):
                grams = []
                for src, r, c in sketches:
                    left = c[layer, pl.ds(2 * m, 2)].reshape(256, 256)
                    right = r[layer, pl.ds(2 * quarter, 2)].reshape(256, 256)
                    grams.append(lax.dot_general(left, right, (((1,), (1,)), ((), ())), preferred_element_type=jnp.float32))
                total = total + grams[0] * grams[1]
            kt[pl.ds(pl.multiple_of(m * 256, 256), 256), lanes] = (total * inv_scale).astype(jnp.bfloat16)
            return 0

        lax.fori_loop(0, 4, block, 0, unroll=True)

    tcopy.wait_send()
    for group in (*zc, *yc.values(), *fc.values(), *xc.values()):
        for c in group:
            c.wait_send()

    def step(p, last=False):
        gathered = [remote(xbuf.at[p, :, jcols], xbuf.at[p, :, jcols], ags.at[p, n], agr.at[p, n], at(dy=dy, dk=dk))
                    for n, (dy, dk) in enumerate(gathers)]
        arrived = {d: c for d, c in zip(gathers, gathered)}

        def pair_of(dy):
            return pl.ds(pl.multiple_of(((y - dy) % 4) * 256, 256), 256)

        for dy in (0, 1, 3):
            for dk in (0, 1):
                if (dy, dk) != (0, 0):
                    arrived[dy, dk].wait_recv()
            term = jnp.dot(xbuf[p, :, pair_of(dy)], kt[pair_of(dy), :], preferred_element_type=jnp.float32)
            acc[...] = term if dy == 0 else acc[...] + term
        for dk in (0, 1):
            arrived[2, dk].wait_recv()
        last_pair = xbuf[p, :, pair_of(2)]
        copies = {}
        for dx in (2, 1, 3, 0):
            lanes = pl.ds(pl.multiple_of(((x + dx) % 4) * 256, 256), 256)
            part = acc[:, lanes] + jnp.dot(last_pair, kt[pair_of(2), lanes], preferred_element_type=jnp.float32)
            for b in range(2):
                rsend[p, dx, b] = part[:, b * 128:(b + 1) * 128].astype(jnp.bfloat16)
            if dx == 0:
                yloc[...] = part
            for n, (ddx, dz) in enumerate(sums):
                if ddx == dx:
                    copies[n] = remote(rsend.at[p, dx, zb + dz * (1 - 2 * zb)], rrecv.at[p, n], rss.at[p, n], rsr.at[p, n],
                                       at(dx=dx, dzb=dz))
                    copies[n].start()
        for c in gathered:
            c.wait_send()
        total = yloc[:, pl.ds(pl.multiple_of(zb * 128, 128), 128)]
        for n in reversed(range(7)):
            copies[n].wait_recv()
            total = total + rrecv[p, n].astype(jnp.float32)
        res[...] = res[...] - RATE * total
        if not last:
            gather(1 - p)
        for c in copies.values():
            c.wait_send()

    def pair(_, carry):
        step(0)
        step(1)
        return carry

    lax.fori_loop(0, ITERS // 2 - 1, pair, 0)
    step(0)
    step(1, last=True)

    sq[...] = jnp.zeros_like(sq)
    sq[pl.ds(half_at, 64), :] = res[...]
    osend[...] = sq[...].T
    for h in range(2):
        for e in range(2):
            n = 2 * h + e
            z_to = 4 * h + 2 * zb + e
            piece = osend.at[pl.ds(h * 64 + e * 32, 32)]

            @pl.when(z_to != z)
            def _():
                remote(piece, orecv.at[q], oss.at[n], osr.at[q], place(x, y, z_to, k)).start()

            @pl.when(z_to == z)
            def _():
                pltpu.make_async_copy(piece, orecv.at[q], osr.at[q]).start()
    for n in range(4):
        pltpu.make_async_copy(osend.at[pl.ds(0, 32)], orecv.at[n], osr.at[n]).wait()
    out[:, 0:128] = orecv[0] + orecv[1]
    out[:, 128:256] = orecv[2] + orecv[3]
    for h in range(2):
        for e in range(2):
            n = 2 * h + e
            z_to = 4 * h + 2 * zb + e
            piece = osend.at[pl.ds(h * 64 + e * 32, 32)]

            @pl.when(z_to != z)
            def _():
                remote(piece, orecv.at[q], oss.at[n], osr.at[q], place(x, y, z_to, k)).wait_send()


def body(act_sketch, grad_sketch, targets):
    layers, examples, width = act_sketch.shape
    inv_scale = 4.0 / (width * math.sqrt(examples * lax.axis_size("row")))
    bf16, f32 = jnp.bfloat16, jnp.float32
    dma = pltpu.SemaphoreType.DMA
    hbm = pl.BlockSpec(memory_space=pltpu.HBM)
    return pl.pallas_call(
        functools.partial(kernel, inv_scale),
        name="descent",
        out_shape=jax.ShapeDtypeStruct((32, 256), f32),
        in_specs=[hbm, hbm, hbm],
        out_specs=pl.BlockSpec(memory_space=pltpu.VMEM),
        scratch_shapes=[
            *[pltpu.VMEM((2, 8, 2, 64, 256), bf16)] * 4,
            pltpu.VMEM((1024, 1024), bf16),
            pltpu.VMEM((2, 64, 1024), bf16),
            pltpu.VMEM((2, 4, 2, 64, 128), bf16),
            pltpu.VMEM((2, 7, 64, 128), bf16),
            pltpu.VMEM((64, 1024), f32),
            pltpu.VMEM((64, 256), f32),
            pltpu.VMEM((64, 128), f32),
            pltpu.VMEM((2, 64, 128), f32),
            pltpu.VMEM((128, 128), f32),
            pltpu.VMEM((128, 128), f32),
            pltpu.VMEM((4, 32, 128), f32),
            dma((4, 2)),
            dma((CHUNKS, 2)), dma((CHUNKS, 2)),
            dma(()), dma(()),
            dma((3, CHUNKS, 2)), dma((3, CHUNKS, 2)),
            dma((3, 1 + CHUNKS, 2)), dma((3, 1 + CHUNKS, 2)),
            dma((4, 1 + CHUNKS, 2)), dma((4, 1 + CHUNKS, 2)),
            dma((2, 7)), dma((2, 7)),
            dma((2, 7)), dma((2, 7)),
            dma((4,)), dma((4,)),
        ],
        compiler_params=pltpu.CompilerParams(collective_id=0, has_side_effects=True, vmem_limit_bytes=40 * 2**20),
    )(*[pltpu.with_memory_space_constraint(v, pltpu.HBM) for v in (act_sketch.reshape(layers, 8, 64, width), grad_sketch.reshape(layers, 8, 64, width),
      targets.reshape(8, 64, targets.shape[1]))])


def solution(mesh):
    return jax.shard_map(
        body,
        mesh=mesh,
        in_specs=(P(None, "row", None), P(None, "row", None), P("row", None)),
        out_specs=P(("row", "col"), None),
        check_vma=False,
    )
```

time: 2480 us -> 106 us (0.04)
  waiting for transfers between devices: 2160 us -> 0 us
  blocking collectives: 267 us -> 0 us
  Pallas kernels: 0 us -> 105 us
    psum x8 -> x0, waiting for transfers between devices: 1550 us -> none  [broadcast(): return lax.psum(kept, axis)]
    reduce_scatter x8 -> x0, waiting for transfers between devices: 607 us -> none  [body(): lax.psum_scatter(partial_value, 'col', scatter_dimension=0, tiled=True)]
    all_gather x8 -> x0, blocking collectives: 267 us -> none  [body(): gathered = lax.all_gather(squashed, 'col', axis=0, tiled=True)]
    pallas_call x0 -> x1, Pallas kernels: none -> 105 us  [body(): pl.pallas_call(functools.partial(kernel, inv_scale), name='descent', out_...]
  transfers between devices with their start and end apart: 16 -> 0, of which waited for: 16 -> 0; matrix products, arithmetic and copies ran while one was open for 0% -> 0% of each run, Pallas kernels for 0% -> 0%
where the time goes in v1:
time: 106 us
  Pallas kernels  105 us (99%)
    pallas_call x1, Pallas kernels, body(): pl.pallas_call(functools.partial(kernel, inv_scale), name='descent', out_...  105 us

profile of v1, /device:TPU:1, one launch (start us, length us, event | category | flops | bytes accessed | tf_op | source)
XLA Modules:
  0.0 106.0 jit_solution(14836479126575935871)
XLA Ops:
  0.0 105.3 %descent.1 = f32[32,256]{1,0:T(8,128)S(1)} custom-call(bf16[2,8,64,256]{3,2,1,0:T(8,128)(2,1)} %bitcast.3, bf16[2,8,64,256]{3,2,1,0:T(8,128)(2,1)} %bitcast.4, f32[8,64,256]{2,1,0:T(8,128)} %bitcast.5), custom_call_target="tpu_custom_call" | custom-call | tf_op jit(solution)/shard_map/descent/pallas_call | solution.py:280
  105.4 0.6 copy.5

commit v2 on v1

--- a/solution.py
+++ b/solution.py
@@ -10,6 +10,7 @@
 
 ITERS = 8
 CHUNKS = 4
+ORDER = ((2,), (3,), (0, 1))
 RATE = 0.05
 MESH = pl.DeviceIdType.MESH
 
@@ -19,7 +20,7 @@
 
 
 def kernel(inv_scale, act, grad, tgt, out, ra, rg, ca, cg, kt, xbuf, rsend, rrecv, acc, yloc, res, tbuf, sq, osend, orecv,
-           lsem, zs, zr, ts, tr, xs, xr, ys, yr, fs, fr, rss, rsr, ags, agr, oss, osr):
+           lsem, zs, zfs, zr, ts, tr, xs, xr, ys, yr, fs, fr, rss, rsr, ags, agr, oss, osr):
     row, col = lax.axis_index("row"), lax.axis_index("col")
     x, zlo = col // 4, col % 4
     hi, y, k = row // 8, (row // 2) % 4, row % 2
@@ -55,13 +56,13 @@
     def greet(device):
         pl.semaphore_signal(barrier, inc=1, device_id=device, device_id_type=MESH)
 
+    for n in range(1, 4):
+        for b in range(2):
+            greet(place(x, y, 2 * ((q + n) % 4) + b, k))
     for dx, dz in sums:
         greet(at(dx=dx, dzb=dz))
     for dy, dk in gathers:
         greet(at(dy=dy, dk=dk))
-    for n in range(1, 4):
-        for b in range(2):
-            greet(place(x, y, 2 * ((q + n) % 4) + b, k))
     pl.semaphore_wait(barrier, len(sums) + len(gathers) + 6)
 
     mirror = place(x, y, 7 - z, k)
@@ -69,14 +70,21 @@
     mcols = pl.ds(pl.multiple_of(((3 - q) // 2) * 128, 128), 128)
     tcopy = remote(tgt.at[s_mirror, :, mcols], tbuf.at[hi], ts, tr, mirror)
     tcopy.start()
-    zc = []
+    outer = zlo % 3 == 0
     mine = pl.ds(2 * x, 2)
     rows_of = [pl.ds(c * (64 // CHUNKS), 64 // CHUNKS) for c in range(CHUNKS)]
+    zc, zf = [], []
     for chunk, i in enumerate(rows_of):
         zc.append([remote(src.at[:, mine, i], r.at[:, mine, hi, i], zs.at[chunk, n], zr.at[chunk, n], mirror)
                    for n, (src, r, c) in enumerate(sketches)])
-    for c in zc[0]:
-        c.start()
+        zf.append([remote(r.at[:, mine, lo, i], r.at[:, mine, lo, i], zfs.at[chunk, n], zr.at[chunk, n], at(dzb=1))
+                   for n, (src, r, c) in enumerate(sketches)])
+
+    @pl.when(outer)
+    def _():
+        for c in (c for group in zc for c in group):
+            c.start()
+
     yc, fc, xc = {}, {}, {}
     everything = pl.ds(0, 64)
 
@@ -110,9 +118,6 @@
             c.start()
 
     columns(0, hi)
-    for chunk in zc[1:]:
-        for c in chunk:
-            c.start()
     forward(0, 0, hi)
 
     tlocal.wait()
@@ -120,33 +125,38 @@
     sq[...] = tbuf[...].reshape(128, 128).T
     half_at = pl.multiple_of((q % 2) * 64, 64)
     res[...] = sq[pl.ds(half_at, 64), :]
-    jcols = pl.ds(pl.multiple_of(j_me * 128, 128), 128)
+    def slot(d):
+        return pl.ds((2 * d[0] + d[1]) * 128, 128)
+
+    def gather_copies(p):
+        return [remote(xbuf.at[p, :, slot((0, 0))], xbuf.at[p, :, slot(d)], ags.at[p, n], agr.at[p, n], at(dy=d[0], dk=d[1]))
+                for n, d in enumerate(gathers)]
 
     def gather(p):
-        xbuf[p, :, jcols] = jnp.tanh(res[...]).astype(jnp.bfloat16)
-        copies = [remote(xbuf.at[p, :, jcols], xbuf.at[p, :, jcols], ags.at[p, n], agr.at[p, n], at(dy=dy, dk=dk))
-                  for n, (dy, dk) in enumerate(gathers)]
-        for c in copies:
+        xbuf[p, :, slot((0, 0))] = jnp.tanh(res[...]).astype(jnp.bfloat16)
+        for c in gather_copies(p):
             c.start()
-        return copies
-
-    first = gather(0)
+
+    gather(0)
 
     for chunk, i in enumerate(rows_of):
         for c in zc[chunk]:
             c.wait_recv()
+
+        @pl.when(outer)
+        def _():
+            for passed in zf[chunk]:
+                passed.start()
+
+        for dx in (2, 1, 3):
+            rows(dx, chunk)
         columns(1 + chunk, lo, i)
-        rows(1, chunk)
-        rows(3, chunk)
-        if chunk:
-            rows(2, chunk - 1)
         forward(0, 1 + chunk, lo, i)
         if chunk == 1:
             for dy in (1, 3, 2):
                 for c in yc[dy, 0]:
                     c.wait_recv()
                 forward(dy, 0, hi)
-    rows(2, CHUNKS - 1)
     for n, (src, r, c) in enumerate(sketches):
         own = pltpu.make_async_copy(r.at[:, s_me, lo], c.at[:, j_me, lo], lsem.at[3, n])
         own.start()
@@ -167,61 +177,60 @@
             for chunk in range(CHUNKS):
                 for c in xc[dx, chunk]:
                     c.wait_recv()
-        quarter = (x - dx) % 4
-        lanes = pl.ds(pl.multiple_of(quarter * 256, 256), 256)
-
-        def block(m, _):
+        to = (4 - dx) % 4
+        lanes = pl.ds(to * 256, 256)
+        right_at = [2 * ((x - dx) % 4) + zb, 2 * ((x - dx) % 4) + 1 - zb]
+        for dy in range(4):
+            left_at = [2 * ((y - dy) % 4) + k, 2 * ((y - dy) % 4) + 1 - k]
             total = jnp.zeros((256, 256), jnp.float32)
             for layer in range(2):
                 grams = []
                 for src, r, c in sketches:
-                    left = c[layer, pl.ds(2 * m, 2)].reshape(256, 256)
-                    right = r[layer, pl.ds(2 * quarter, 2)].reshape(256, 256)
+                    left = jnp.concatenate([c[layer, j].reshape(128, 256) for j in left_at], axis=0)
+                    right = jnp.concatenate([r[layer, j].reshape(128, 256) for j in right_at], axis=0)
                     grams.append(lax.dot_general(left, right, (((1,), (1,)), ((), ())), preferred_element_type=jnp.float32))
                 total = total + grams[0] * grams[1]
-            kt[pl.ds(pl.multiple_of(m * 256, 256), 256), lanes] = (total * inv_scale).astype(jnp.bfloat16)
-            return 0
-
-        lax.fori_loop(0, 4, block, 0, unroll=True)
+            kt[pl.ds(dy * 256, 256), lanes] = (total * inv_scale).astype(jnp.bfloat16)
 
     tcopy.wait_send()
-    for group in (*zc, *yc.values(), *fc.values(), *xc.values()):
+
+    @pl.when(outer)
+    def _():
+        for c in (c for group in (*zc, *zf) for c in group):
+            c.wait_send()
+
+    for group in (*yc.values(), *fc.values(), *xc.values()):
         for c in group:
             c.wait_send()
 
     def step(p, last=False):
-        gathered = [remote(xbuf.at[p, :, jcols], xbuf.at[p, :, jcols], ags.at[p, n], agr.at[p, n], at(dy=dy, dk=dk))
-                    for n, (dy, dk) in enumerate(gathers)]
-        arrived = {d: c for d, c in zip(gathers, gathered)}
-
-        def pair_of(dy):
-            return pl.ds(pl.multiple_of(((y - dy) % 4) * 256, 256), 256)
-
-        for dy in (0, 1, 3):
-            for dk in (0, 1):
-                if (dy, dk) != (0, 0):
-                    arrived[dy, dk].wait_recv()
-            term = jnp.dot(xbuf[p, :, pair_of(dy)], kt[pair_of(dy), :], preferred_element_type=jnp.float32)
-            acc[...] = term if dy == 0 else acc[...] + term
-        for dk in (0, 1):
-            arrived[2, dk].wait_recv()
-        last_pair = xbuf[p, :, pair_of(2)]
+        gathered = gather_copies(p)
+        arrived = dict(zip(gathers, gathered))
+        for d in ((0, 1), (1, 0), (1, 1), (3, 0), (3, 1)):
+            arrived[d].wait_recv()
+        term = jnp.dot(xbuf[p, :, 0:512], kt[0:512, :], preferred_element_type=jnp.float32)
+        acc[...] = term + jnp.dot(xbuf[p, :, 768:1024], kt[768:1024, :], preferred_element_type=jnp.float32)
+        for d in ((2, 0), (2, 1)):
+            arrived[d].wait_recv()
+        last_pair = xbuf[p, :, 512:768]
         copies = {}
-        for dx in (2, 1, 3, 0):
-            lanes = pl.ds(pl.multiple_of(((x + dx) % 4) * 256, 256), 256)
-            part = acc[:, lanes] + jnp.dot(last_pair, kt[pair_of(2), lanes], preferred_element_type=jnp.float32)
-            for b in range(2):
-                rsend[p, dx, b] = part[:, b * 128:(b + 1) * 128].astype(jnp.bfloat16)
-            if dx == 0:
-                yloc[...] = part
-            for n, (ddx, dz) in enumerate(sums):
-                if ddx == dx:
-                    copies[n] = remote(rsend.at[p, dx, zb + dz * (1 - 2 * zb)], rrecv.at[p, n], rss.at[p, n], rsr.at[p, n],
-                                       at(dx=dx, dzb=dz))
+        for group in ORDER:
+            first, count = group[0] * 256, len(group) * 256
+            part = acc[:, first:first + count] + jnp.dot(
+                last_pair, kt[512:768, first:first + count], preferred_element_type=jnp.float32)
+            if 0 in group:
+                yloc[...] = part[:, 0:128]
+            for at_n, (dx, dz) in enumerate((dx, dz) for dx in group for dz in range(2)):
+                if (dx, dz) != (0, 0):
+                    n = sums.index((dx, dz))
+                    rsend[p, n] = part[:, at_n * 128:(at_n + 1) * 128].astype(jnp.bfloat16)
+                    copies[n] = remote(rsend.at[p, n], rrecv.at[p, n], rss.at[p, n], rsr.at[p, n], at(dx=dx, dzb=dz))
+            for n in sorted(copies):
+                if sums[n][0] in group:
                     copies[n].start()
         for c in gathered:
             c.wait_send()
-        total = yloc[:, pl.ds(pl.multiple_of(zb * 128, 128), 128)]
+        total = yloc[...]
         for n in reversed(range(7)):
             copies[n].wait_recv()
             total = total + rrecv[p, n].astype(jnp.float32)
@@ -287,17 +296,17 @@
             *[pltpu.VMEM((2, 8, 2, 64, 256), bf16)] * 4,
             pltpu.VMEM((1024, 1024), bf16),
             pltpu.VMEM((2, 64, 1024), bf16),
-            pltpu.VMEM((2, 4, 2, 64, 128), bf16),
+            pltpu.VMEM((2, 7, 64, 128), bf16),
             pltpu.VMEM((2, 7, 64, 128), bf16),
             pltpu.VMEM((64, 1024), f32),
-            pltpu.VMEM((64, 256), f32),
+            pltpu.VMEM((64, 128), f32),
             pltpu.VMEM((64, 128), f32),
             pltpu.VMEM((2, 64, 128), f32),
             pltpu.VMEM((128, 128), f32),
             pltpu.VMEM((128, 128), f32),
             pltpu.VMEM((4, 32, 128), f32),
             dma((4, 2)),
-            dma((CHUNKS, 2)), dma((CHUNKS, 2)),
+            dma((CHUNKS, 2)), dma((CHUNKS, 2)), dma((CHUNKS, 2)),
             dma(()), dma(()),
             dma((3, CHUNKS, 2)), dma((3, CHUNKS, 2)),
             dma((3, 1 + CHUNKS, 2)), dma((3, 1 + CHUNKS, 2)),

time: 106 us -> 103 us (0.972)
  Pallas kernels: 105 us -> 102 us
    pallas_call x1, Pallas kernels: 105 us -> 102 us  [body(): pl.pallas_call(functools.partial(kernel, inv_scale), name='descent', out_...]
where the time goes in v2:
time: 103 us
  Pallas kernels  102 us (99%)
    pallas_call x1, Pallas kernels, body(): pl.pallas_call(functools.partial(kernel, inv_scale), name='descent', out_...  102 us

profile of v2, /device:TPU:1, one launch (start us, length us, event | category | flops | bytes accessed | tf_op | source)
XLA Modules:
  0.0 102.5 jit_solution(13534123199488507223)
XLA Ops:
  0.0 101.9 %descent.1 = f32[32,256]{1,0:T(8,128)S(1)} custom-call(bf16[2,8,64,256]{3,2,1,0:T(8,128)(2,1)} %bitcast.3, bf16[2,8,64,256]{3,2,1,0:T(8,128)(2,1)} %bitcast.4, f32[8,64,256]{2,1,0:T(8,128)} %bitcast.5), custom_call_target="tpu_custom_call" | custom-call | tf_op jit(solution)/shard_map/descent/pallas_call | solution.py:289
  101.9 0.6 copy.5

commit v3 on v2

--- a/solution.py
+++ b/solution.py
@@ -10,7 +10,7 @@
 
 ITERS = 8
 CHUNKS = 4
-ORDER = ((2,), (3,), (0, 1))
+HALVES = 2
 RATE = 0.05
 MESH = pl.DeviceIdType.MESH
 
@@ -19,7 +19,7 @@
     return ((z // 4) * 8 + y * 2 + k, x * 4 + z % 4)
 
 
-def kernel(inv_scale, act, grad, tgt, out, ra, rg, ca, cg, kt, xbuf, rsend, rrecv, acc, yloc, res, tbuf, sq, osend, orecv,
+def kernel(inv_scale, act, grad, tgt, out, ra, rg, ca, cg, kt, xbuf, rsend, rrecv, yloc, res, tbuf, sq, osend, orecv,
            lsem, zs, zfs, zr, ts, tr, xs, xr, ys, yr, fs, fr, rss, rsr, ags, agr, oss, osr):
     row, col = lax.axis_index("row"), lax.axis_index("col")
     x, zlo = col // 4, col % 4
@@ -124,20 +124,21 @@
     tcopy.wait_recv()
     sq[...] = tbuf[...].reshape(128, 128).T
     half_at = pl.multiple_of((q % 2) * 64, 64)
-    res[...] = sq[pl.ds(half_at, 64), :]
+    res[...] = sq[pl.ds(half_at, 64), :].reshape(res.shape)
     def slot(d):
         return pl.ds((2 * d[0] + d[1]) * 128, 128)
 
-    def gather_copies(p):
-        return [remote(xbuf.at[p, :, slot((0, 0))], xbuf.at[p, :, slot(d)], ags.at[p, n], agr.at[p, n], at(dy=d[0], dk=d[1]))
-                for n, d in enumerate(gathers)]
-
-    def gather(p):
-        xbuf[p, :, slot((0, 0))] = jnp.tanh(res[...]).astype(jnp.bfloat16)
-        for c in gather_copies(p):
+    def gather_copies(p, h):
+        return [remote(xbuf.at[p, h, :, slot((0, 0))], xbuf.at[p, h, :, slot(d)], ags.at[p, h, n], agr.at[p, h, n],
+                       at(dy=d[0], dk=d[1])) for n, d in enumerate(gathers)]
+
+    def gather(p, h):
+        xbuf[p, h, :, slot((0, 0))] = jnp.tanh(res[h]).astype(jnp.bfloat16)
+        for c in gather_copies(p, h):
             c.start()
 
-    gather(0)
+    for h in range(HALVES):
+        gather(0, h)
 
     for chunk, i in enumerate(rows_of):
         for c in zc[chunk]:
@@ -192,52 +193,34 @@
                 total = total + grams[0] * grams[1]
             kt[pl.ds(dy * 256, 256), lanes] = (total * inv_scale).astype(jnp.bfloat16)
 
-    tcopy.wait_send()
-
-    @pl.when(outer)
-    def _():
-        for c in (c for group in (*zc, *zf) for c in group):
+    def step(p, last=False):
+        gathered, copies = [], []
+        for h in range(HALVES):
+            gathered.append(gather_copies(p, h))
+            for c in reversed(gathered[h]):
+                c.wait_recv()
+            part = jnp.dot(xbuf[p, h], kt[...], preferred_element_type=jnp.float32)
+            yloc[h] = part[:, 0:128]
+            copies.append([])
+            for n, (dx, dz) in enumerate(sums):
+                lane = (2 * dx + dz) * 128
+                rsend[p, h, n] = part[:, lane:lane + 128].astype(jnp.bfloat16)
+                copies[h].append(remote(
+                    rsend.at[p, h, n], rrecv.at[p, h, n], rss.at[p, h, n], rsr.at[p, h, n], at(dx=dx, dzb=dz)))
+            for c in copies[h]:
+                c.start()
+        for c in (c for group in gathered for c in group):
             c.wait_send()
-
-    for group in (*yc.values(), *fc.values(), *xc.values()):
-        for c in group:
-            c.wait_send()
-
-    def step(p, last=False):
-        gathered = gather_copies(p)
-        arrived = dict(zip(gathers, gathered))
-        for d in ((0, 1), (1, 0), (1, 1), (3, 0), (3, 1)):
-            arrived[d].wait_recv()
-        term = jnp.dot(xbuf[p, :, 0:512], kt[0:512, :], preferred_element_type=jnp.float32)
-        acc[...] = term + jnp.dot(xbuf[p, :, 768:1024], kt[768:1024, :], preferred_element_type=jnp.float32)
-        for d in ((2, 0), (2, 1)):
-            arrived[d].wait_recv()
-        last_pair = xbuf[p, :, 512:768]
-        copies = {}
-        for group in ORDER:
-            first, count = group[0] * 256, len(group) * 256
-            part = acc[:, first:first + count] + jnp.dot(
-                last_pair, kt[512:768, first:first + count], preferred_element_type=jnp.float32)
-            if 0 in group:
-                yloc[...] = part[:, 0:128]
-            for at_n, (dx, dz) in enumerate((dx, dz) for dx in group for dz in range(2)):
-                if (dx, dz) != (0, 0):
-                    n = sums.index((dx, dz))
-                    rsend[p, n] = part[:, at_n * 128:(at_n + 1) * 128].astype(jnp.bfloat16)
-                    copies[n] = remote(rsend.at[p, n], rrecv.at[p, n], rss.at[p, n], rsr.at[p, n], at(dx=dx, dzb=dz))
-            for n in sorted(copies):
-                if sums[n][0] in group:
-                    copies[n].start()
-        for c in gathered:
-            c.wait_send()
-        total = yloc[...]
-        for n in reversed(range(7)):
-            copies[n].wait_recv()
-            total = total + rrecv[p, n].astype(jnp.float32)
-        res[...] = res[...] - RATE * total
-        if not last:
-            gather(1 - p)
-        for c in copies.values():
+        for h in range(HALVES):
+            for c in reversed(copies[h]):
+                c.wait_recv()
+            total = yloc[h]
+            for n in range(7):
+                total = total + rrecv[p, h, n].astype(jnp.float32)
+            res[h] = res[h] - RATE * total
+            if not last:
+                gather(1 - p, h)
+        for c in (c for group in copies for c in group):
             c.wait_send()
 
     def pair(_, carry):
@@ -250,7 +233,7 @@
     step(1, last=True)
 
     sq[...] = jnp.zeros_like(sq)
-    sq[pl.ds(half_at, 64), :] = res[...]
+    sq[pl.ds(half_at, 64), :] = res[...].reshape(64, 128)
     osend[...] = sq[...].T
     for h in range(2):
         for e in range(2):
@@ -265,6 +248,17 @@
             @pl.when(z_to == z)
             def _():
                 pltpu.make_async_copy(piece, orecv.at[q], osr.at[q]).start()
+    tcopy.wait_send()
+
+    @pl.when(outer)
+    def _():
+        for c in (c for group in (*zc, *zf) for c in group):
+            c.wait_send()
+
+    for group in (*yc.values(), *fc.values(), *xc.values()):
+        for c in group:
+            c.wait_send()
+
     for n in range(4):
         pltpu.make_async_copy(osend.at[pl.ds(0, 32)], orecv.at[n], osr.at[n]).wait()
     out[:, 0:128] = orecv[0] + orecv[1]
@@ -295,12 +289,11 @@
         scratch_shapes=[
             *[pltpu.VMEM((2, 8, 2, 64, 256), bf16)] * 4,
             pltpu.VMEM((1024, 1024), bf16),
-            pltpu.VMEM((2, 64, 1024), bf16),
-            pltpu.VMEM((2, 7, 64, 128), bf16),
-            pltpu.VMEM((2, 7, 64, 128), bf16),
-            pltpu.VMEM((64, 1024), f32),
-            pltpu.VMEM((64, 128), f32),
-            pltpu.VMEM((64, 128), f32),
+            pltpu.VMEM((2, HALVES, 64 // HALVES, 1024), bf16),
+            pltpu.VMEM((2, HALVES, 7, 64 // HALVES, 128), bf16),
+            pltpu.VMEM((2, HALVES, 7, 64 // HALVES, 128), bf16),
+            pltpu.VMEM((HALVES, 64 // HALVES, 128), f32),
+            pltpu.VMEM((HALVES, 64 // HALVES, 128), f32),
             pltpu.VMEM((2, 64, 128), f32),
             pltpu.VMEM((128, 128), f32),
             pltpu.VMEM((128, 128), f32),
@@ -311,8 +304,8 @@
             dma((3, CHUNKS, 2)), dma((3, CHUNKS, 2)),
             dma((3, 1 + CHUNKS, 2)), dma((3, 1 + CHUNKS, 2)),
             dma((4, 1 + CHUNKS, 2)), dma((4, 1 + CHUNKS, 2)),
-            dma((2, 7)), dma((2, 7)),
-            dma((2, 7)), dma((2, 7)),
+            dma((2, HALVES, 7)), dma((2, HALVES, 7)),
+            dma((2, HALVES, 7)), dma((2, HALVES, 7)),
             dma((4,)), dma((4,)),
         ],
         compiler_params=pltpu.CompilerParams(collective_id=0, has_side_effects=True, vmem_limit_bytes=40 * 2**20),

time: 103 us -> 101 us (0.981)
  Pallas kernels: 102 us -> 100 us
    pallas_call x1, Pallas kernels: 102 us -> 100 us  [body(): pl.pallas_call(functools.partial(kernel, inv_scale), name='descent', out_...]
where the time goes in v3:
time: 101 us
  Pallas kernels  100 us (99%)
    pallas_call x1, Pallas kernels, body(): pl.pallas_call(functools.partial(kernel, inv_scale), name='descent', out_...  100 us

profile of v3, /device:TPU:1, one launch (start us, length us, event | category | flops | bytes accessed | tf_op | source)
XLA Modules:
  0.0 101.1 jit_solution(17962996272704099185)
XLA Ops:
  0.0 100.5 %descent.1 = f32[32,256]{1,0:T(8,128)S(1)} custom-call(bf16[2,8,64,256]{3,2,1,0:T(8,128)(2,1)} %bitcast.3, bf16[2,8,64,256]{3,2,1,0:T(8,128)(2,1)} %bitcast.4, f32[8,64,256]{2,1,0:T(8,128)} %bitcast.5), custom_call_target="tpu_custom_call" | custom-call | tf_op jit(solution)/shard_map/descent/pallas_call | solution.py:283
  100.5 0.6 copy.5

commit v4 on v3

--- a/solution.py
+++ b/solution.py
@@ -9,8 +9,9 @@
 from jax.sharding import PartitionSpec as P
 
 ITERS = 8
-CHUNKS = 4
-HALVES = 2
+SIZES = (16, 16, 16, 16)
+CHUNKS = len(SIZES)
+PARTS = 4
 RATE = 0.05
 MESH = pl.DeviceIdType.MESH
 
@@ -72,7 +73,7 @@
     tcopy.start()
     outer = zlo % 3 == 0
     mine = pl.ds(2 * x, 2)
-    rows_of = [pl.ds(c * (64 // CHUNKS), 64 // CHUNKS) for c in range(CHUNKS)]
+    rows_of = [pl.ds(sum(SIZES[:c]), SIZES[c]) for c in range(CHUNKS)]
     zc, zf = [], []
     for chunk, i in enumerate(rows_of):
         zc.append([remote(src.at[:, mine, i], r.at[:, mine, hi, i], zs.at[chunk, n], zr.at[chunk, n], mirror)
@@ -137,7 +138,7 @@
         for c in gather_copies(p, h):
             c.start()
 
-    for h in range(HALVES):
+    for h in range(PARTS):
         gather(0, h)
 
     for chunk, i in enumerate(rows_of):
@@ -195,7 +196,7 @@
 
     def step(p, last=False):
         gathered, copies = [], []
-        for h in range(HALVES):
+        for h in range(PARTS):
             gathered.append(gather_copies(p, h))
             for c in reversed(gathered[h]):
                 c.wait_recv()
@@ -211,7 +212,7 @@
                 c.start()
         for c in (c for group in gathered for c in group):
             c.wait_send()
-        for h in range(HALVES):
+        for h in range(PARTS):
             for c in reversed(copies[h]):
                 c.wait_recv()
             total = yloc[h]
@@ -289,11 +290,11 @@
         scratch_shapes=[
             *[pltpu.VMEM((2, 8, 2, 64, 256), bf16)] * 4,
             pltpu.VMEM((1024, 1024), bf16),
-            pltpu.VMEM((2, HALVES, 64 // HALVES, 1024), bf16),
-            pltpu.VMEM((2, HALVES, 7, 64 // HALVES, 128), bf16),
-            pltpu.VMEM((2, HALVES, 7, 64 // HALVES, 128), bf16),
-            pltpu.VMEM((HALVES, 64 // HALVES, 128), f32),
-            pltpu.VMEM((HALVES, 64 // HALVES, 128), f32),
+            pltpu.VMEM((2, PARTS, 64 // PARTS, 1024), bf16),
+            pltpu.VMEM((2, PARTS, 7, 64 // PARTS, 128), bf16),
+            pltpu.VMEM((2, PARTS, 7, 64 // PARTS, 128), bf16),
+            pltpu.VMEM((PARTS, 64 // PARTS, 128), f32),
+            pltpu.VMEM((PARTS, 64 // PARTS, 128), f32),
             pltpu.VMEM((2, 64, 128), f32),
             pltpu.VMEM((128, 128), f32),
             pltpu.VMEM((128, 128), f32),
@@ -304,8 +305,8 @@
             dma((3, CHUNKS, 2)), dma((3, CHUNKS, 2)),
             dma((3, 1 + CHUNKS, 2)), dma((3, 1 + CHUNKS, 2)),
             dma((4, 1 + CHUNKS, 2)), dma((4, 1 + CHUNKS, 2)),
-            dma((2, HALVES, 7)), dma((2, HALVES, 7)),
-            dma((2, HALVES, 7)), dma((2, HALVES, 7)),
+            dma((2, PARTS, 7)), dma((2, PARTS, 7)),
+            dma((2, PARTS, 7)), dma((2, PARTS, 7)),
             dma((4,)), dma((4,)),
         ],
         compiler_params=pltpu.CompilerParams(collective_id=0, has_side_effects=True, vmem_limit_bytes=40 * 2**20),

time: 101 us -> 101 us (level)
  no operation moved by 1% of the time
where the time goes in v4:
time: 101 us
  Pallas kernels  100 us (99%)
    pallas_call x1, Pallas kernels, body(): pl.pallas_call(functools.partial(kernel, inv_scale), name='descent', out_...  100 us

profile of v4, /device:TPU:1, one launch (start us, length us, event | category | flops | bytes accessed | tf_op | source)
XLA Modules:
  0.0 100.7 jit_solution(6079523698301075646)
XLA Ops:
  0.0 100.1 %descent.1 = f32[32,256]{1,0:T(8,128)S(1)} custom-call(bf16[2,8,64,256]{3,2,1,0:T(8,128)(2,1)} %bitcast.3, bf16[2,8,64,256]{3,2,1,0:T(8,128)(2,1)} %bitcast.4, f32[8,64,256]{2,1,0:T(8,128)} %bitcast.5), custom_call_target="tpu_custom_call" | custom-call | tf_op jit(solution)/shard_map/descent/pallas_call | solution.py:284
  100.1 0.6 copy.5

commit v5 on v4

--- a/solution.py
+++ b/solution.py
@@ -12,6 +12,7 @@
 SIZES = (16, 16, 16, 16)
 CHUNKS = len(SIZES)
 PARTS = 4
+ORDER = ((2, 3), (0, 1))
 RATE = 0.05
 MESH = pl.DeviceIdType.MESH
 
@@ -28,7 +29,6 @@
     z = hi * 4 + zlo
     zb = z % 2
     q = z // 2
-    lo = 1 - hi
     s_me = 2 * x + zb
     j_me = 2 * y + k
     sketches = ((act, ra, ca), (grad, rg, cg))
@@ -42,10 +42,10 @@
 
     local = []
     for n, (src, r, c) in enumerate(sketches):
-        local.append(pltpu.make_async_copy(src, r.at[:, :, hi], lsem.at[0, n]))
-        local.append(pltpu.make_async_copy(src.at[:, s_me], c.at[:, j_me, hi], lsem.at[1, n]))
+        local.append(pltpu.make_async_copy(src, r.at[:, :, 0], lsem.at[0, n]))
+        local.append(pltpu.make_async_copy(src.at[:, s_me], c.at[:, j_me, 0], lsem.at[1, n]))
     tcols = pl.ds(pl.multiple_of((q // 2) * 128, 128), 128)
-    tlocal = pltpu.make_async_copy(tgt.at[s_me, :, tcols], tbuf.at[hi], lsem.at[2, 0])
+    tlocal = pltpu.make_async_copy(tgt.at[s_me, :, tcols], tbuf.at[0], lsem.at[2, 0])
     for c in local:
         c.start()
     tlocal.start()
@@ -69,16 +69,16 @@
     mirror = place(x, y, 7 - z, k)
     s_mirror = 2 * x + 1 - zb
     mcols = pl.ds(pl.multiple_of(((3 - q) // 2) * 128, 128), 128)
-    tcopy = remote(tgt.at[s_mirror, :, mcols], tbuf.at[hi], ts, tr, mirror)
+    tcopy = remote(tgt.at[s_mirror, :, mcols], tbuf.at[1], ts, tr, mirror)
     tcopy.start()
     outer = zlo % 3 == 0
     mine = pl.ds(2 * x, 2)
     rows_of = [pl.ds(sum(SIZES[:c]), SIZES[c]) for c in range(CHUNKS)]
     zc, zf = [], []
     for chunk, i in enumerate(rows_of):
-        zc.append([remote(src.at[:, mine, i], r.at[:, mine, hi, i], zs.at[chunk, n], zr.at[chunk, n], mirror)
+        zc.append([remote(src.at[:, mine, i], r.at[:, mine, 1, i], zs.at[chunk, n], zr.at[chunk, n], mirror)
                    for n, (src, r, c) in enumerate(sketches)])
-        zf.append([remote(r.at[:, mine, lo, i], r.at[:, mine, lo, i], zfs.at[chunk, n], zr.at[chunk, n], at(dzb=1))
+        zf.append([remote(r.at[:, mine, 1, i], r.at[:, mine, 1, i], zfs.at[chunk, n], zr.at[chunk, n], at(dzb=1))
                    for n, (src, r, c) in enumerate(sketches)])
 
     @pl.when(outer)
@@ -94,7 +94,7 @@
         fc[dy, part] = []
         for n, (src, r, c) in enumerate(sketches):
             if dy == 0:
-                source = src.at[:, s_me, i] if part == 0 else r.at[:, s_me, lo, i]
+                source = src.at[:, s_me, i] if part == 0 else r.at[:, s_me, 1, i]
             else:
                 source = c.at[:, j, half, i]
             fc[dy, part].append(remote(source, c.at[:, j, half, i], fs.at[dy, part, n], fr.at[dy, part, n], at(dk=1)))
@@ -105,7 +105,7 @@
         for dy in (2, 1, 3):
             yc[dy, part] = []
             for n, (src, r, c) in enumerate(sketches):
-                source = src.at[:, s_me, i] if part == 0 else r.at[:, s_me, lo, i]
+                source = src.at[:, s_me, i] if part == 0 else r.at[:, s_me, 1, i]
                 yc[dy, part].append(remote(
                     source, c.at[:, j_me, half, i], ys.at[dy - 1, part, n], yr.at[dy - 1, part, n], at(dy=dy)))
             for c in yc[dy, part]:
@@ -113,13 +113,13 @@
 
     def rows(dx, chunk):
         i = rows_of[chunk]
-        xc[dx, chunk] = [remote(r.at[:, mine, lo, i], r.at[:, mine, lo, i], xs.at[dx - 1, chunk, n], xr.at[dx - 1, chunk, n],
+        xc[dx, chunk] = [remote(r.at[:, mine, 1, i], r.at[:, mine, 1, i], xs.at[dx - 1, chunk, n], xr.at[dx - 1, chunk, n],
                                 at(dx=dx)) for n, (src, r, c) in enumerate(sketches)]
         for c in xc[dx, chunk]:
             c.start()
 
-    columns(0, hi)
-    forward(0, 0, hi)
+    columns(0, 0)
+    forward(0, 0, 0)
 
     tlocal.wait()
     tcopy.wait_recv()
@@ -152,47 +152,69 @@
 
         for dx in (2, 1, 3):
             rows(dx, chunk)
-        columns(1 + chunk, lo, i)
-        forward(0, 1 + chunk, lo, i)
+        columns(1 + chunk, 1, i)
+        forward(0, 1 + chunk, 1, i)
         if chunk == 1:
             for dy in (1, 3, 2):
                 for c in yc[dy, 0]:
                     c.wait_recv()
-                forward(dy, 0, hi)
+                forward(dy, 0, 0)
     for n, (src, r, c) in enumerate(sketches):
-        own = pltpu.make_async_copy(r.at[:, s_me, lo], c.at[:, j_me, lo], lsem.at[3, n])
+        own = pltpu.make_async_copy(r.at[:, s_me, 1], c.at[:, j_me, 1], lsem.at[3, n])
         own.start()
         local.append(own)
     for chunk, i in enumerate(rows_of):
         for dy in (1, 3, 2):
             for c in yc[dy, 1 + chunk]:
                 c.wait_recv()
-            forward(dy, 1 + chunk, lo, i)
+            forward(dy, 1 + chunk, 1, i)
     for c in local:
         c.wait()
     for group in fc.values():
         for c in group:
             c.wait_recv()
 
-    for dx in (0, 1, 3, 2):
-        if dx:
+    first_lanes = lax.broadcasted_iota(jnp.int32, (256, 128), 1) < 64
+
+    def products(half, dy, places):
+        left_at = [2 * ((y - dy) % 4) + k, 2 * ((y - dy) % 4) + 1 - k]
+        total = jnp.zeros((256, 64 * len(places)), jnp.float32)
+        for layer in range(2):
+            grams = []
+            for src, r, c in sketches:
+                left = jnp.concatenate([c[layer, j].reshape(128, 256) for j in left_at], axis=0)
+                right = jnp.concatenate(
+                    [r[layer, 2 * ((x + dx) % 4) + (zb if dz == 0 else 1 - zb), half] for dx, dz in places], axis=0)
+                grams.append(lax.dot_general(left, right, (((1,), (1,)), ((), ())), preferred_element_type=jnp.float32))
+            total = total + grams[0] * grams[1]
+        return total * inv_scale
+
+    def place_own(dxs):
+        for dy in range(4):
+            block = products(0, dy, [(dx, dz) for dx in dxs for dz in range(2)])
+            for m, dx in enumerate(dxs):
+                pair = block[:, m * 128:(m + 1) * 128]
+                kt[dy * 256:(dy + 1) * 256, dx * 256:dx * 256 + 128] = pair.astype(jnp.bfloat16)
+                kt[dy * 256:(dy + 1) * 256, dx * 256 + 128:dx * 256 + 256] = pltpu.roll(pair, 64, 1).astype(jnp.bfloat16)
+
+    def place_other(dxs):
+        for dy in range(4):
+            block = products(1, dy, [(dx, dz) for dx in dxs for dz in range(2)])
+            for m, dx in enumerate(dxs):
+                pair = block[:, m * 128:(m + 1) * 128]
+                for dz, value in ((0, pltpu.roll(pair, 64, 1)), (1, pair)):
+                    at_k = kt.at[pl.ds(dy * 256, 256), pl.ds(dx * 256 + dz * 128, 128)]
+                    at_k[...] = jnp.where(first_lanes, at_k[...].astype(jnp.float32), value).astype(jnp.bfloat16)
+
+    place_own((0, 1))
+    place_own((2, 3))
+    place_other((0,))
+    for dxs in ((1, 3, 2),):
+        for dx in dxs:
             for chunk in range(CHUNKS):
                 for c in xc[dx, chunk]:
                     c.wait_recv()
-        to = (4 - dx) % 4
-        lanes = pl.ds(to * 256, 256)
-        right_at = [2 * ((x - dx) % 4) + zb, 2 * ((x - dx) % 4) + 1 - zb]
-        for dy in range(4):
-            left_at = [2 * ((y - dy) % 4) + k, 2 * ((y - dy) % 4) + 1 - k]
-            total = jnp.zeros((256, 256), jnp.float32)
-            for layer in range(2):
-                grams = []
-                for src, r, c in sketches:
-                    left = jnp.concatenate([c[layer, j].reshape(128, 256) for j in left_at], axis=0)
-                    right = jnp.concatenate([r[layer, j].reshape(128, 256) for j in right_at], axis=0)
-                    grams.append(lax.dot_general(left, right, (((1,), (1,)), ((), ())), preferred_element_type=jnp.float32))
-                total = total + grams[0] * grams[1]
-            kt[pl.ds(dy * 256, 256), lanes] = (total * inv_scale).astype(jnp.bfloat16)
+        place_other([(4 - dx) % 4 for dx in dxs])
 
     def step(p, last=False):
         gathered, copies = [], []
@@ -200,16 +222,21 @@
             gathered.append(gather_copies(p, h))
             for c in reversed(gathered[h]):
                 c.wait_recv()
-            part = jnp.dot(xbuf[p, h], kt[...], preferred_element_type=jnp.float32)
-            yloc[h] = part[:, 0:128]
-            copies.append([])
-            for n, (dx, dz) in enumerate(sums):
-                lane = (2 * dx + dz) * 128
-                rsend[p, h, n] = part[:, lane:lane + 128].astype(jnp.bfloat16)
-                copies[h].append(remote(
-                    rsend.at[p, h, n], rrecv.at[p, h, n], rss.at[p, h, n], rsr.at[p, h, n], at(dx=dx, dzb=dz)))
-            for c in copies[h]:
-                c.start()
+            copies.append([None] * len(sums))
+            for dxs in ORDER:
+                part = jnp.dot(xbuf[p, h], kt[:, dxs[0] * 256:(dxs[-1] + 1) * 256], preferred_element_type=jnp.float32)
+                for m, (dx, dz) in enumerate((dx, dz) for dx in dxs for dz in range(2)):
+                    piece = part[:, m * 128:(m + 1) * 128]
+                    if (dx, dz) == (0, 0):
+                        yloc[h] = piece
+                        continue
+                    n = sums.index((dx, dz))
+                    rsend[p, h, n] = piece.astype(jnp.bfloat16)
+                    copies[h][n] = remote(
+                        rsend.at[p, h, n], rrecv.at[p, h, n], rss.at[p, h, n], rsr.at[p, h, n], at(dx=dx, dzb=dz))
+                for n, (dx, dz) in enumerate(sums):
+                    if dx in dxs:
+                        copies[h][n].start()
         for c in (c for group in gathered for c in group):
             c.wait_send()
         for h in range(PARTS):
@@ -239,7 +266,7 @@
     for h in range(2):
         for e in range(2):
             n = 2 * h + e
-            z_to = 4 * h + 2 * zb + e
+            z_to = 4 * (hi if h == 0 else 1 - hi) + 2 * zb + e
             piece = osend.at[pl.ds(h * 64 + e * 32, 32)]
 
             @pl.when(z_to != z)
@@ -267,7 +294,7 @@
     for h in range(2):
         for e in range(2):
             n = 2 * h + e
-            z_to = 4 * h + 2 * zb + e
+            z_to = 4 * (hi if h == 0 else 1 - hi) + 2 * zb + e
             piece = osend.at[pl.ds(h * 64 + e * 32, 32)]
 
             @pl.when(z_to != z)

time: 101 us -> 99.5 us (0.985)
  Pallas kernels: 100 us -> 98.8 us
    pallas_call x1, Pallas kernels: 100 us -> 98.8 us  [body(): pl.pallas_call(functools.partial(kernel, inv_scale), name='descent', out_...]
where the time goes in v5:
time: 99.5 us; the launch traced here: 99.4 us
  Pallas kernels  98.8 us (99%)
    pallas_call x1, Pallas kernels, body(): pl.pallas_call(functools.partial(kernel, inv_scale), name='descent', out_...  98.8 us

profile of v5, /device:TPU:1, one launch (start us, length us, event | category | flops | bytes accessed | tf_op | source)
XLA Modules:
  0.0 99.4 jit_solution(15076894348409202817)
XLA Ops:
  0.0 98.8 %descent.1 = f32[32,256]{1,0:T(8,128)S(1)} custom-call(bf16[2,8,64,256]{3,2,1,0:T(8,128)(2,1)} %bitcast.3, bf16[2,8,64,256]{3,2,1,0:T(8,128)(2,1)} %bitcast.4, f32[8,64,256]{2,1,0:T(8,128)} %bitcast.5), custom_call_target="tpu_custom_call" | custom-call | tf_op jit(solution)/shard_map/descent/pallas_call | solution.py:311
  98.8 0.6 copy.5

commit v6 on v5

--- a/solution.py
+++ b/solution.py
@@ -60,11 +60,13 @@
     for n in range(1, 4):
         for b in range(2):
             greet(place(x, y, 2 * ((q + n) % 4) + b, k))
-    for dx, dz in sums:
+    near = [(dx, dz) for dx, dz in sums if 0 in (dx, dz)]
+    beside = [(dy, dk) for dy, dk in gathers if 0 in (dy, dk)]
+    for dx, dz in near:
         greet(at(dx=dx, dzb=dz))
-    for dy, dk in gathers:
+    for dy, dk in beside:
         greet(at(dy=dy, dk=dk))
-    pl.semaphore_wait(barrier, len(sums) + len(gathers) + 6)
+    pl.semaphore_wait(barrier, len(near) + len(beside) + 6)
 
     mirror = place(x, y, 7 - z, k)
     s_mirror = 2 * x + 1 - zb
@@ -138,8 +140,6 @@
         for c in gather_copies(p, h):
             c.start()
 
-    for h in range(PARTS):
-        gather(0, h)
 
     for chunk, i in enumerate(rows_of):
         for c in zc[chunk]:
@@ -159,6 +159,8 @@
                 for c in yc[dy, 0]:
                     c.wait_recv()
                 forward(dy, 0, 0)
+            for h in range(PARTS):
+                gather(0, h)
     for n, (src, r, c) in enumerate(sketches):
         own = pltpu.make_async_copy(r.at[:, s_me, 1], c.at[:, j_me, 1], lsem.at[3, n])
         own.start()

time: 99.5 us -> 99.6 us (level)
  no operation moved by 1% of the time
where the time goes in v6:
time: 99.6 us; the launch traced here: 99.5 us
  Pallas kernels  98.9 us (99%)
    pallas_call x1, Pallas kernels, body(): pl.pallas_call(functools.partial(kernel, inv_scale), name='descent', out_...  98.9 us

profile of v6, /device:TPU:1, one launch (start us, length us, event | category | flops | bytes accessed | tf_op | source)
XLA Modules:
  0.0 99.5 jit_solution(8137948605197999864)
XLA Ops:
  0.0 98.9 %descent.1 = f32[32,256]{1,0:T(8,128)S(1)} custom-call(bf16[2,8,64,256]{3,2,1,0:T(8,128)(2,1)} %bitcast.3, bf16[2,8,64,256]{3,2,1,0:T(8,128)(2,1)} %bitcast.4, f32[8,64,256]{2,1,0:T(8,128)} %bitcast.5), custom_call_target="tpu_custom_call" | custom-call | tf_op jit(solution)/shard_map/descent/pallas_call | solution.py:313
  98.9 0.6 copy.5
